TPU v7x, 256 devices: a whole 4x4x8 slice. The times are simulated.
256 devices in a mesh: day: 4 (over x), sta: 64 (over y, z, core).
Axes of the slice: x: 4, y: 4, z: 8, core: 2. Of those that a mesh axis runs over, the one named last changes fastest.
Arguments:
- raw_spectra: bfloat16 [96, 8192, 2, 128], P('day', 'sta'), may hold values from -6 to 6
- station_block: int32 [8192], replicated, may hold values from 0 to 63, as said below
- pair_listed: int32 [64, 3], P('sta'), may hold values 0 or 1
Outputs:
- stacks: bfloat16 [64, 3, 2, 128, 128, 128], P('sta', None, None, 'day')
Inputs may be any that keep to these rules, and one draw needn't show every extreme that they name: `station_block`: every block holds exactly 128 stations; of the 128 consecutive stations of one ingest shard at most 3 belong to one block, and every shard reaches that most.
All inputs are finite; a program needn't handle non-finite values. No bound on the sum of `pair_listed` on one device may be relied on, other than what follows from the above.
Results may differ from a plain program's by a relative error of at most 0.012.
Values may be sent and summed in bfloat16 or wider, within the bound.
A program may use at most 128 MiB of HBM per device.

v0:
```python
import jax
import jax.numpy as jnp
from jax import lax
from jax.sharding import PartitionSpec as P


def shifted(block, axis, distance):
    devices = range(lax.axis_size(axis))
    route = [((i - distance) % len(devices), i) for i in devices]
    return lax.ppermute(block, axis, route)


def for_sending(value):

    def short(part):
        return part.astype(jnp.bfloat16) if part.dtype == jnp.float32 else part

    return jax.tree.map(short, value)


def correlate(first, second):
    real_b = second[:, :, :, 0, :]
    imag_b = second[:, :, :, 1, :]
    swapped = jnp.stack([imag_b, -real_b], axis=3)
    paired = jnp.stack([second, swapped], axis=4)
    return jnp.einsum("igscf,jgscpf->gpfij", first, paired, preferred_element_type=jnp.float32)


def neighbours(field, count):
    result = [field]
    for offset in range(1, count):
        result.append(shifted(field, "sta", -offset))
    return result


def local(raw_spectra, station_block, pair_listed):
    blocks = lax.axis_size("sta")
    groups = lax.axis_size("day")
    me_block = lax.axis_index("sta")
    segments = raw_spectra.shape[0]
    block_size = raw_spectra.shape[1]
    bins = raw_spectra.shape[3]
    window = pair_listed.shape[1]
    most = block_size // blocks + 1
    values = raw_spectra.astype(jnp.float32)
    power = values[:, :, 0, :] ** 2 + values[:, :, 1, :] ** 2
    level = jnp.mean(power, axis=-1, keepdims=True)
    white = (values / jnp.sqrt(power + level + 1e-05)[:, :, None, :]).astype(jnp.bfloat16)
    by_station = jnp.transpose(white, (1, 0, 2, 3))
    labels = jnp.arange(blocks, dtype=jnp.int32)
    full_hot = (station_block[:, None] == labels[None, :]).astype(jnp.int32)
    counts = jnp.sum(full_hot.reshape(blocks, block_size, blocks), axis=1)
    before = (labels[:, None] < labels[None, :]).astype(jnp.int32)
    earlier = jnp.sum(before[:, :, None] * counts[:, None, :], axis=0)
    own_blocks = lax.dynamic_slice_in_dim(station_block, me_block * block_size, block_size)
    own_hot = (own_blocks[:, None] == labels[None, :]).astype(jnp.int32)
    rank_in = jnp.sum((jnp.cumsum(own_hot, axis=0) - own_hot) * own_hot, axis=1)
    outgoing = jnp.zeros((blocks, most, segments, 2, bins), jnp.bfloat16)
    outgoing = outgoing.at[own_blocks, rank_in].set(by_station)
    incoming = lax.all_to_all(outgoing, "sta", split_axis=0, concat_axis=0, tiled=True)
    source_counts = lax.dynamic_slice_in_dim(counts, me_block, 1, axis=1)
    source_start = lax.dynamic_slice_in_dim(earlier, me_block, 1, axis=1)
    slot_rank = jnp.arange(most, dtype=jnp.int32)[None, :]
    target = jnp.where(slot_rank < source_counts, source_start + slot_rank, block_size).reshape(-1)
    arranged = jnp.zeros((block_size, segments, 2, bins), jnp.bfloat16)
    arranged = arranged.at[target].set(
        incoming.reshape(blocks * most, segments, 2, bins), mode="drop"
    )
    own_field = arranged[:, None]
    scale = 1.0 / jnp.sqrt(jnp.float32(segments * groups))
    weights = pair_listed[0].astype(jnp.float32)
    others = neighbours(own_field, window)
    terms = []
    for offset in range(window):
        product = correlate(own_field, others[offset])[0]
        terms.append(product * weights[offset])
    summed = jax.tree.map(
        lambda part: part.astype(jnp.float32),
        lax.psum_scatter(for_sending(tuple(terms)), "day", scatter_dimension=1, tiled=True),
    )
    return (jnp.stack(summed) * scale).astype(jnp.bfloat16)[None]


def solution(mesh):
    in_specs = (P("day", "sta", None, None), P(), P("sta", None))
    out_specs = P("sta", None, None, "day", None, None)
    return jax.shard_map(local, mesh=mesh, in_specs=in_specs, out_specs=out_specs, check_vma=False)
```

profile of v0, /device:TPU:1, one launch (start us, length us, event | category | flops | bytes accessed | tf_op | source)
XLA Modules:
  0.0 436.3 jit_solution(8639674949959267416)
XLA Ops:
  6.5 0.8 dynamic_slice.11
  7.3 0.1 fusion.12
  7.4 0.2 reduce_window_sum.11
  7.6 0.2 select_reduce_fusion
  7.7 0.8 fusion.16
  8.5 2.7 convert_element_type.76
  11.2 23.7 %fusion.18 = (f32[24,128]{1,0:T(8,128)S(1)}, f32[24,128,1,128]{3,2,1,0:T(1,128)S(1)}) fusion(f32[24,128,2,128]{3,2,1,0:T(2,128)S(1)} %convert_element_type.76), kind=kLoop, calls=%fused_computation.54 | loop fusion | flops 1569792 | bytes 4730880 | tf_op jit(solution)/shard_map/reduce_sum | solution.py:47
  34.9 4.5 %add_sqrt_fusion = f32[24,128,1,128]{3,2,1,0:T(1,128)S(1)} fusion(f32[24,128,1,128]{3,2,1,0:T(1,128)S(1)} %get-tuple-element.6, f32[24,128]{1,0:T(8,128)S(1)} %broadcast_multiply_fusion), kind=kLoop, calls=%fused_computation.29 | loop fusion | flops 786432 | bytes 3158016 | tf_op jit(solution)/shard_map/sqrt | solution.py:48
  39.4 1.7 fusion.11
  41.1 1.8 copy.33
  42.9 1.7 broadcast_in_dim.17
  44.6 17.0 %scatter_fusion = bf16[64,3,24,2,128]{4,2,3,1,0:T(8,128)(2,1)} fusion(bf16[64,3,24,2,128]{4,2,3,1,0:T(8,128)(2,1)} %broadcast_in_dim.17, s32[128]{0:T(128)S(1)} %fusion.16, bf16[128,24,2,128]{3,1,2,0:T(8,128)(2,1)S(1)} %copy.33), kind=kCustom, calls=%fused_computation | custom fusion | bytes 4719616 | tf_op jit(solution)/shard_map/scatter | solution.py:59
  61.6 13.3 %all-to-all-start = ((bf16[64,3,24,2,128]{4,2,3,1,0:T(8,128)(2,1)}), bf16[64,3,24,2,128]{4,2,3,1,0:T(8,128)(2,1)S(1)}, u32[]{:S(2)}, u32[]{:S(2)}) async-start(bf16[64,3,24,2,128]{4,2,3,1,0:T(8,128)(2,1)} %scatter_fusion), calls=%async_computation | async-start | bytes 4718592 | tf_op jit(solution)/shard_map/all_to_all | solution.py:60
  74.9 0.0 reduce-scatter.4.cloned.1.call-start
  75.0 1.2 convert_reduce_fusion
  76.1 0.7 multiply_reduce_fusion
  76.8 0.2 dynamic-slice_reduce_fusion
  77.0 0.1 add_select_fusion
  77.1 0.1 select_n.47
  77.3 0.6 fusion.23
  77.9 53.6 %all-to-all-done = bf16[64,3,24,2,128]{4,2,3,1,0:T(8,128)(2,1)S(1)} async-done(((bf16[64,3,24,2,128]{4,2,3,1,0:T(8,128)(2,1)}), bf16[64,3,24,2,128]{4,2,3,1,0:T(8,128)(2,1)S(1)}, u32[]{:S(2)}, u32[]{:S(2)}) %all-to-all-start) | async-done | bytes 2359328 | tf_op jit(solution)/shard_map/all_to_all | solution.py:60
  131.5 1.4 copy-done
  132.9 0.2 broadcast_in_dim.13
  133.1 17.4 %scatter_fusion.1 = bf16[128,24,2,128]{3,1,2,0:T(8,128)(2,1)S(1)} fusion(bf16[128,24,2,128]{3,1,2,0:T(8,128)(2,1)S(1)} %broadcast_in_dim.13, s32[192]{0:T(256)S(1)} %bitcast.103, bf16[192,24,2,128]{3,1,2,0:T(8,128)(2,1)} %bitcast.91), kind=kCustom, calls=%fused_computation.1 | custom fusion | bytes 7078656 | tf_op jit(solution)/shard_map/scatter | solution.py:66
  150.6 1.5 copy.34
  152.0 1.3 fusion.20
  153.3 2.2 copy.42
  155.6 1.6 maximum_bitcast_fusion.4
  157.2 0.3 copy-done.2
  157.4 5.6 %fusion.3 = bf16[2,128,128,128]{2,3,0,1:T(8,128)(2,1)} fusion(f32[]{:T(128)} %bitcast.15, bf16[128,24,2,128,1]{0,1,2,4,3:T(8,128)(2,1)S(1)} %copy-done.2, bf16[128,1,24,2,1,128]{0,2,3,4,5,1:T(8,128)(2,1)S(1)} %maximum_bitcast_fusion.4, bf16[128,1,24,2,1,128]{0,2,3,4,5,1:T(8,128)(2,1)S(1)} %bitcast.93), kind=kOutput, calls=%fused_computation.9 | convolution fusion | flops 412614656 | bytes 13107204 | tf_op jit(solution)/shard_map/igscf,jgscpf->gpfij/dot_general | solution.py:26
  163.0 0.0 reduce-scatter.4.cloned.1.call-update
  163.0 0.0 reduce-scatter.6.cloned.1.call-start
  163.1 0.4 collective-permute-start
  163.5 19.9 %collective-permute-done = bf16[128,1,24,2,128]{0,2,3,4,1:T(8,128)(2,1)S(1)} collective-permute-done((bf16[128,1,24,2,128]{0,2,3,4,1:T(8,128)(2,1)S(1)}, bf16[128,1,24,2,128]{0,2,3,4,1:T(8,128)(2,1)S(1)}, u32[]{:S(2)}, u32[]{:S(2)}) %collective-permute-start) | collective-permute-done | bytes 1572896 | tf_op jit(solution)/shard_map/ppermute | solution.py:10
  183.4 0.2 fusion.21
  183.6 0.1 maximum_bitcast_fusion.5
  183.7 5.4 %fusion.4 = bf16[2,128,128,128]{2,3,0,1:T(8,128)(2,1)} fusion(f32[]{:T(128)} %bitcast.26, bf16[128,24,2,128,1]{0,1,2,4,3:T(8,128)(2,1)S(1)} %copy-done.2, bf16[128,1,24,2,1,128]{0,2,3,5,4,1:T(8,128)(2,1)S(1)} %maximum_bitcast_fusion.5, bf16[128,1,24,2,1,128]{0,2,3,5,4,1:T(8,128)(2,1)S(1)} %bitcast.101), kind=kOutput, calls=%fused_computation.10 | convolution fusion | flops 412614656 | bytes 13107204 | tf_op jit(solution)/shard_map/igscf,jgscpf->gpfij/dot_general | solution.py:26
  189.1 0.0 reduce-scatter.8.cloned.1.call-start
  189.1 3.8 collective-permute-start.1
  193.0 32.1 %collective-permute-done.1 = bf16[128,1,24,2,128]{0,2,3,4,1:T(8,128)(2,1)S(1)} collective-permute-done((bf16[128,1,24,2,128]{0,2,3,4,1:T(8,128)(2,1)S(1)}, bf16[128,1,24,2,128]{0,2,3,4,1:T(8,128)(2,1)S(1)}, u32[]{:S(2)}, u32[]{:S(2)}) %collective-permute-start.1) | collective-permute-done | bytes 1572896 | tf_op jit(solution)/shard_map/ppermute | solution.py:10
  225.1 0.2 fusion.22
  225.3 0.1 maximum_bitcast_fusion.6
  225.4 5.5 %fusion.5 = bf16[2,128,128,128]{2,3,0,1:T(8,128)(2,1)} fusion(f32[]{:T(128)} %bitcast.37, bf16[128,24,2,128,1]{0,1,2,4,3:T(8,128)(2,1)S(1)} %copy-done.2, bf16[128,1,24,2,1,128]{0,2,3,5,4,1:T(8,128)(2,1)S(1)} %maximum_bitcast_fusion.6, bf16[128,1,24,2,1,128]{0,2,3,5,4,1:T(8,128)(2,1)S(1)} %bitcast.100), kind=kOutput, calls=%fused_computation.11 | convolution fusion | flops 412614656 | bytes 13107204 | tf_op jit(solution)/shard_map/igscf,jgscpf->gpfij/dot_general | solution.py:26
  230.9 11.9 %reduce-scatter.4.cloned.1.call-done = bf16[2,32,128,128]{2,3,0,1:T(8,128)(2,1)} async-done(((bf16[2,128,128,128]{2,3,0,1:T(8,128)(2,1)}), bf16[2,32,128,128]{2,3,0,1:T(8,128)(2,1)}) %reduce-scatter.4.cloned.1.call-update) | async-done | bytes 2097168 | tf_op jit(solution)/shard_map/reduce_scatter | solution.py:79
  242.8 85.5 %reduce-scatter.6.cloned.1.call-done = bf16[2,32,128,128]{2,3,0,1:T(8,128)(2,1)} async-done(((bf16[2,128,128,128]{2,3,0,1:T(8,128)(2,1)}), bf16[2,32,128,128]{2,3,0,1:T(8,128)(2,1)}) %reduce-scatter.6.cloned.1.call-update) | async-done | bytes 2097168 | tf_op jit(solution)/shard_map/reduce_scatter | solution.py:79
  328.3 85.5 %reduce-scatter.8.cloned.1.call-done = bf16[2,32,128,128]{2,3,0,1:T(8,128)(2,1)} async-done(((bf16[2,128,128,128]{2,3,0,1:T(8,128)(2,1)}), bf16[2,32,128,128]{2,3,0,1:T(8,128)(2,1)}) %reduce-scatter.8.cloned.1.call-update) | async-done | bytes 2097168 | tf_op jit(solution)/shard_map/reduce_scatter | solution.py:79
  413.7 7.4 %multiply_convert_fusion = bf16[1,3,2,32,128,128]{4,5,2,3,1,0:T(8,128)(2,1)} fusion(bf16[1,1,2,32,128,128]{4,5,2,3,1,0:T(8,128)(2,1)} %bitcast.99, bf16[1,1,2,32,128,128]{4,5,2,3,1,0:T(8,128)(2,1)} %bitcast.98, bf16[1,1,2,32,128,128]{4,5,2,3,1,0:T(8,128)(2,1)} %bitcast.97), kind=kLoop, calls=%fused_computation.8 | loop fusion | flops 15728640 | bytes 12582912 | tf_op jit(solution)/shard_map/convert_element_type | solution.py:81
  421.2 8.6 %copy.41 = bf16[1,3,2,32,128,128]{5,4,3,2,1,0:T(8,128)(2,1)} copy(bf16[1,3,2,32,128,128]{4,5,2,3,1,0:T(8,128)(2,1)} %multiply_convert_fusion) | data formatting | bytes 12582912 | tf_op jit(solution)/shard_map/convert_element_type | solution.py:81
  (14 shorter events, 0.1 us)
Async XLA Ops:
  34.9 4.5 %copy-start.1 = (bf16[24,128,2,128]{3,2,1,0:T(2,128)(2,1)S(1)}, bf16[24,128,2,128]{3,2,1,0:T(2,128)(2,1)}, u32[]{:S(2)}) copy-start(bf16[24,128,2,128]{3,2,1,0:T(2,128)(2,1)} %param.3) | copy-start | bytes 4718596
  61.6 13.4 %copy-start.3 = (s32[8192]{0:T(1024)S(1)}, s32[8192]{0:T(1024)}, u32[]{:S(2)}) copy-start(s32[8192]{0:T(1024)} %param.4) | copy-start | bytes 98308
  61.6 15.6 %copy-start.4 = (s32[1,3]{1,0:T(1,128)S(1)}, s32[1,3]{1,0:T(1,128)}, u32[]{:S(2)}) copy-start(s32[1,3]{1,0:T(1,128)} %param.5) | copy-start | bytes 40
  61.6 69.9 %all-to-all-start = ((bf16[64,3,24,2,128]{4,2,3,1,0:T(8,128)(2,1)}), bf16[64,3,24,2,128]{4,2,3,1,0:T(8,128)(2,1)S(1)}, u32[]{:S(2)}, u32[]{:S(2)}) async-start(bf16[64,3,24,2,128]{4,2,3,1,0:T(8,128)(2,1)} %scatter_fusion), calls=%async_computation | async-start | bytes 4718592 | tf_op jit(solution)/shard_map/all_to_all | solution.py:60
  74.9 167.9 %reduce-scatter.4.cloned.1.call-start = ((), (), s32[]{:S(2)}) async-start(), calls=%async_computation.4 | async-start | bytes 10485760 | tf_op jit(solution)/shard_map/reduce_scatter | solution.py:79
  131.5 1.4 copy-start
  155.6 1.9 copy-start.2
  163.0 165.2 %reduce-scatter.6.cloned.1.call-start = ((), (), s32[]{:S(2)}) async-start(), calls=%async_computation.5 | async-start | bytes 10485760 | tf_op jit(solution)/shard_map/reduce_scatter | solution.py:79
  163.1 20.3 %collective-permute-start = (bf16[128,1,24,2,128]{0,2,3,4,1:T(8,128)(2,1)S(1)}, bf16[128,1,24,2,128]{0,2,3,4,1:T(8,128)(2,1)S(1)}, u32[]{:S(2)}, u32[]{:S(2)}) collective-permute-start(bf16[128,1,24,2,128]{0,2,3,4,1:T(8,128)(2,1)S(1)} %bitcast.94), channel_id=1, source_target_pairs={{1,0},{2,1},{3,2},{4,3},{5,4},{6,5},{7,6},{8,7},{9,8},{10,9},{11,1... | collective-permute-start | bytes 4718600 | tf_op jit(solution)/shard_map/ppermute | solution.py:10
  189.1 224.6 %reduce-scatter.8.cloned.1.call-start = ((), (), s32[]{:S(2)}) async-start(), calls=%async_computation.6 | async-start | bytes 10485760 | tf_op jit(solution)/shard_map/reduce_scatter | solution.py:79
  189.1 36.0 %collective-permute-start.1 = (bf16[128,1,24,2,128]{0,2,3,4,1:T(8,128)(2,1)S(1)}, bf16[128,1,24,2,128]{0,2,3,4,1:T(8,128)(2,1)S(1)}, u32[]{:S(2)}, u32[]{:S(2)}) collective-permute-start(bf16[128,1,24,2,128]{0,2,3,4,1:T(8,128)(2,1)S(1)} %bitcast.95), channel_id=1, source_target_pairs={{2,0},{3,1},{4,2},{5,3},{6,4},{7,5},{8,6},{9,7},{10,8},{11,9},{12,... | collective-permute-start | bytes 4718600 | tf_op jit(solution)/shard_map/ppermute | solution.py:10
Sparse Core Ops, SparseCore 0:
  163.2 79.5 reduce-scatter.3
  245.4 82.8 reduce-scatter.5
  330.9 82.8 reduce-scatter.7
where the time goes:
time: 438 us; the launch traced here: 436 us
  waiting for transfers between devices  289 us (66%)
  local copies, waits for them, and re-layouts  53.8 us (12%)
  other arithmetic  46.6 us (11%)
  starting transfers between devices  17.6 us (4%)
  matrix products  16.4 us (4%)
  between operations  13.3 us (3%)
    reduce_scatter x3, waiting for transfers between devices, local(): lax.psum_scatter(for_sending(tuple(terms)), 'day', scatter_dimension=1, t...  183 us
    all_to_all x1, waiting for transfers between devices, local(): lax.all_to_all(outgoing, 'sta', split_axis=0, concat_axis=0, tiled=True)  53.6 us
    ppermute x2, waiting for transfers between devices, shifted(): return lax.ppermute(block, axis, route)  52.1 us
    reduce_sum x1, other arithmetic, local(): level = jnp.mean(power, axis=-1, keepdims=True)  23.7 us
    scatter x3, local copies, waits for them, and re-layouts, local(): arranged.at[target]  21.1 us
    scatter x1, local copies, waits for them, and re-layouts, local(): outgoing = outgoing.at[own_blocks, rank_in].set(by_station)  17 us
    dot_general x3, matrix products, correlate(): jnp.einsum('igscf,jgscpf->gpfij', first, paired, preferred_element_type=j...  16.4 us
    all_to_all x1, starting transfers between devices, local(): lax.all_to_all(outgoing, 'sta', split_axis=0, concat_axis=0, tiled=True)  13.3 us
  transfers between devices with their start and end apart: 6, of which 6 were waited for; matrix products, arithmetic and copies ran while one was open for 3% of the time, Pallas kernels for 0%

commit v1 on v0

v1 whole, which is shorter than its diff:
```python
import jax
import jax.numpy as jnp
from jax import lax
from jax.sharding import PartitionSpec as P


def shifted(block, axis, distance):
    devices = range(lax.axis_size(axis))
    route = [((i - distance) % len(devices), i) for i in devices]
    return lax.ppermute(block, axis, route)


def correlate(first, second):
    swapped = jnp.stack([second[:, :, 1], -second[:, :, 0]], axis=2)
    paired = jnp.stack([second, swapped], axis=3)
    return jnp.einsum("iscf,jscpf->pfij", first, paired, preferred_element_type=jnp.float32)


def local(raw_spectra, station_block, pair_listed):
    blocks = lax.axis_size("sta")
    groups = lax.axis_size("day")
    me_block = lax.axis_index("sta")
    segments, block_size, _, bins = raw_spectra.shape
    window = pair_listed.shape[1]
    most = 3
    share = bins // groups
    rows = segments * 2 * share // 128
    values = raw_spectra.astype(jnp.float32)
    power = values[:, :, 0, :] ** 2 + values[:, :, 1, :] ** 2
    level = jnp.mean(power, axis=-1, keepdims=True)
    white = (values / jnp.sqrt(power + level + 1e-05)[:, :, None, :]).astype(jnp.bfloat16)
    by_owner = jnp.transpose(white.reshape(segments, block_size, 2, groups, share), (3, 1, 0, 2, 4))
    by_owner = by_owner.reshape(groups, block_size, rows, 128)
    by_day = lax.all_to_all(by_owner, "day", split_axis=0, concat_axis=0, tiled=True)
    by_station = jnp.transpose(by_day, (1, 0, 2, 3)).reshape(block_size, groups * rows, 128)
    labels = jnp.arange(blocks, dtype=jnp.int32)
    full_hot = (station_block[:, None] == labels[None, :]).astype(jnp.int32)
    counts = jnp.sum(full_hot.reshape(blocks, block_size, blocks), axis=1)
    before = (labels[:, None] < labels[None, :]).astype(jnp.int32)
    earlier = jnp.sum(before[:, :, None] * counts[:, None, :], axis=0)
    own_blocks = lax.dynamic_slice_in_dim(station_block, me_block * block_size, block_size)
    own_hot = (own_blocks[:, None] == labels[None, :]).astype(jnp.int32)
    rank_in = jnp.sum((jnp.cumsum(own_hot, axis=0) - own_hot) * own_hot, axis=1)
    outgoing = jnp.zeros((blocks, most, groups * rows, 128), jnp.bfloat16)
    outgoing = outgoing.at[own_blocks, rank_in].set(by_station)
    incoming = lax.all_to_all(outgoing, "sta", split_axis=0, concat_axis=0, tiled=True)
    source_counts = lax.dynamic_slice_in_dim(counts, me_block, 1, axis=1)
    source_start = lax.dynamic_slice_in_dim(earlier, me_block, 1, axis=1)
    slot_rank = jnp.arange(most, dtype=jnp.int32)[None, :]
    target = jnp.where(slot_rank < source_counts, source_start + slot_rank, block_size).reshape(-1)
    arranged = jnp.zeros((block_size, groups * rows, 128), jnp.bfloat16)
    arranged = arranged.at[target].set(incoming.reshape(blocks * most, groups * rows, 128), mode="drop")
    scale = 1.0 / jnp.sqrt(jnp.float32(segments * groups))
    weights = pair_listed[0].astype(jnp.float32)
    fields = [arranged] + [shifted(arranged, "sta", -offset) for offset in range(1, window)]
    fields = [f.reshape(block_size, groups * segments, 2, share) for f in fields]
    results = []
    for offset in range(window):
        product = correlate(fields[0], fields[offset])
        results.append((product * (weights[offset] * scale)).astype(jnp.bfloat16))
    return jnp.stack(results)[None]


def solution(mesh):
    in_specs = (P("day", "sta", None, None), P(), P("sta", None))
    out_specs = P("sta", None, None, "day", None, None)
    return jax.shard_map(local, mesh=mesh, in_specs=in_specs, out_specs=out_specs, check_vma=False)
```

time: 438 us -> 219 us (0.50)
  the two profiles are of different devices: /device:TPU:1 before, /device:TPU:8 now
where the time goes in v1:
time: 219 us; the launch traced here: 217 us
  waiting for transfers between devices  105 us (48%)
  local copies, waits for them, and re-layouts  70.1 us (32%)
  starting transfers between devices  20.3 us (9%)
  other arithmetic  9.8 us (4%)
  matrix products  9.41 us (4%)
  between operations  2.19 us (1%)
    all_to_all x1, waiting for transfers between devices, local(): lax.all_to_all(outgoing, 'sta', split_axis=0, concat_axis=0, tiled=True)  52.5 us
    ppermute x2, waiting for transfers between devices, shifted(): return lax.ppermute(block, axis, route)  32.9 us
    all_to_all x1, waiting for transfers between devices, local(): lax.all_to_all(by_owner, 'day', split_axis=0, concat_axis=0, tiled=True)  20.1 us
    scatter x2, local copies, waits for them, and re-layouts, local(): arranged.at[target]  18.7 us
    scatter x1, local copies, waits for them, and re-layouts, local(): outgoing = outgoing.at[own_blocks, rank_in].set(by_station)  17 us
    all_to_all x1, starting transfers between devices, local(): lax.all_to_all(outgoing, 'sta', split_axis=0, concat_axis=0, tiled=True)  12.1 us
    dot_general x3, matrix products, correlate(): jnp.einsum('iscf,jscpf->pfij', first, paired, preferred_element_type=jnp....  9.41 us
    unnamed x20, local copies, waits for them, and re-layouts  8.8 us
  transfers between devices with their start and end apart: 4, of which 4 were waited for; matrix products, arithmetic and copies ran while one was open for 9% of the time, Pallas kernels for 0%

profile of v1, /device:TPU:8, one launch (start us, length us, event | category | flops | bytes accessed | tf_op | source)
XLA Modules:
  0.0 217.3 jit_solution(7056083948187597610)
XLA Ops:
  0.0 3.6 %copy.70 = bf16[24,128,2,128]{1,3,2,0:T(8,128)(2,1)S(1)} copy(bf16[24,128,2,128]{3,2,1,0:T(2,128)(2,1)} %param.3) | data formatting | bytes 3145728 | tf_op args[0]
  3.6 0.4 convert_element_type.45
  4.0 0.3 fusion.28
  4.3 0.6 sqrt_bitcast_fusion
  5.0 0.6 divide_convert_fusion
  5.5 1.6 copy.71
  7.1 4.4 %all-to-all-start = ((bf16[4,128,12,128]{1,3,2,0:T(8,128)(2,1)}), bf16[4,128,12,128]{1,3,2,0:T(8,128)(2,1)S(1)}, u32[]{:S(2)}, u32[]{:S(2)}) async-start(bf16[4,128,12,128]{1,3,2,0:T(8,128)(2,1)} %bitcast.8), calls=%async_computation | async-start | bytes 3145728 | tf_op jit(solution)/shard_map/all_to_all | solution.py:34
  11.7 0.2 reduce_window_sum.11
  12.2 20.1 %all-to-all-done = bf16[4,128,12,128]{1,3,2,0:T(8,128)(2,1)S(1)} async-done(((bf16[4,128,12,128]{1,3,2,0:T(8,128)(2,1)}), bf16[4,128,12,128]{1,3,2,0:T(8,128)(2,1)S(1)}, u32[]{:S(2)}, u32[]{:S(2)}) %all-to-all-start) | async-done | bytes 1572896 | tf_op jit(solution)/shard_map/all_to_all | solution.py:34
  32.3 1.0 copy.73
  33.3 1.7 broadcast_in_dim.17
  35.0 17.0 %scatter_fusion = bf16[64,3,48,128]{3,2,1,0:T(8,128)(2,1)} fusion(bf16[64,3,48,128]{3,2,1,0:T(8,128)(2,1)} %broadcast_in_dim.17, s32[128]{0:T(128)S(1)} %fusion.33, bf16[128,48,128]{2,1,0:T(8,128)(2,1)S(1)} %copy.73), kind=kCustom, calls=%fused_computation | custom fusion | bytes 4719616 | tf_op jit(solution)/shard_map/scatter | solution.py:45
  52.0 12.1 %all-to-all-start.1 = ((bf16[64,3,48,128]{3,2,1,0:T(8,128)(2,1)}), bf16[64,3,48,128]{3,2,1,0:T(8,128)(2,1)S(1)}, u32[]{:S(2)}, u32[]{:S(2)}) async-start(bf16[64,3,48,128]{3,2,1,0:T(8,128)(2,1)} %scatter_fusion), calls=%async_computation.1 | async-start | bytes 4718592 | tf_op jit(solution)/shard_map/all_to_all | solution.py:46
  64.1 1.2 convert_reduce_fusion
  65.2 0.7 multiply_reduce_fusion
  66.0 0.2 dynamic-slice_reduce_fusion
  66.4 52.5 %all-to-all-done.1 = bf16[64,3,48,128]{3,2,1,0:T(8,128)(2,1)S(1)} async-done(((bf16[64,3,48,128]{3,2,1,0:T(8,128)(2,1)}), bf16[64,3,48,128]{3,2,1,0:T(8,128)(2,1)S(1)}, u32[]{:S(2)}, u32[]{:S(2)}) %all-to-all-start.1) | async-done | bytes 2359328 | tf_op jit(solution)/shard_map/all_to_all | solution.py:46
  118.9 1.4 copy-done.1
  120.3 0.2 broadcast_in_dim.13
  120.5 17.5 %scatter_fusion.1 = bf16[128,48,128]{2,1,0:T(8,128)(2,1)S(1)} fusion(bf16[128,48,128]{2,1,0:T(8,128)(2,1)S(1)} %broadcast_in_dim.13, s32[192]{0:T(256)S(1)} %bitcast.93, bf16[192,48,128]{2,1,0:T(8,128)(2,1)} %bitcast.89), kind=kCustom, calls=%fused_computation.1 | custom fusion | bytes 7078656 | tf_op jit(solution)/shard_map/scatter | solution.py:52
  138.0 1.5 collective-permute-start
  139.6 0.7 fusion.40
  142.1 1.1 copy.74
  143.3 2.2 %collective-permute-start.1 = (bf16[128,48,128]{2,1,0:T(8,128)(2,1)S(1)}, bf16[128,48,128]{2,1,0:T(8,128)(2,1)}, u32[]{:S(2)}, u32[]{:S(2)}) collective-permute-start(bf16[128,48,128]{2,1,0:T(8,128)(2,1)S(1)} %scatter_fusion.1), channel_id=1, source_target_pairs={{2,0},{3,1},{4,2},{5,3},{6,4},{7,5},{8,6},{9,7},{10,8},{11,9},{12,... | collective-permute-start | bytes 4718600 | tf_op jit(solution)/shard_map/ppermute | solution.py:10
  145.5 1.0 copy.78
  146.5 0.3 fusion.37
  146.8 0.3 copy.107
  147.1 0.4 copy_negate_fusion.2
  147.6 4.0 %fusion.15 = bf16[1,2,32,128,128]{3,4,1,2,0:T(8,128)(2,1)} fusion(f32[]{:T(128)} %bitcast.18, bf16[128,96,2,1,32]{0,1,2,3,4:T(8,128)(2,1)S(1)} %maximum_bitcast_fusion.1, bf16[128,96,2,1,32]{0,1,2,3,4:T(8,128)(2,1)S(1)} %copy.78, bf16[128,96,2,32,1]{0,3,2,1,4:T(8,128)(2,1)S(1)} %bitcast.82), kind=kOutput, calls=%fused_computation.22 | convolution fusion | flops 406323200 | bytes 6815748 | tf_op jit(solution)/shard_map/iscf,jscpf->pfij/dot_general | solution.py:16
  151.6 18.5 %collective-permute-done = bf16[128,48,128]{2,1,0:T(8,128)(2,1)} collective-permute-done((bf16[128,48,128]{2,1,0:T(8,128)(2,1)S(1)}, bf16[128,48,128]{2,1,0:T(8,128)(2,1)}, u32[]{:S(2)}, u32[]{:S(2)}) %collective-permute-start) | collective-permute-done | bytes 1572896 | tf_op jit(solution)/shard_map/ppermute | solution.py:10
  170.1 2.8 %copy.80 = bf16[128,48,128]{0,2,1:T(8,128)(2,1)} copy(bf16[128,48,128]{2,1,0:T(8,128)(2,1)} %collective-permute-done) | data formatting | bytes 3145728 | tf_op jit(solution)/shard_map/ppermute | solution.py:10
  172.9 3.7 %copy.84 = bf16[128,96,2,1,32]{0,1,2,3,4:T(8,128)(2,1)} copy(bf16[128,96,2,1,32]{0,4,2,1,3:T(8,128)(2,1)} %bitcast.85) | data formatting | bytes 3145728 | tf_op jit(solution)/shard_map/stack;reshape | solution.py:15
  176.6 0.3 fusion.38
  176.9 1.2 copy.109
  178.1 1.2 copy_negate_fusion.1
  179.3 14.4 %collective-permute-done.1 = bf16[128,48,128]{2,1,0:T(8,128)(2,1)} collective-permute-done((bf16[128,48,128]{2,1,0:T(8,128)(2,1)S(1)}, bf16[128,48,128]{2,1,0:T(8,128)(2,1)}, u32[]{:S(2)}, u32[]{:S(2)}) %collective-permute-start.1) | collective-permute-done | bytes 1572896 | tf_op jit(solution)/shard_map/ppermute | solution.py:10
  193.8 2.1 copy.86
  195.9 1.0 copy.90
  196.9 0.3 fusion.39
  197.2 0.3 copy.111
  197.5 0.4 copy_negate_fusion
  197.9 0.4 copy-done.2
  198.3 0.2 copy-done.3
  198.9 1.3 copy-done.5
  200.1 2.7 %fusion.16 = bf16[1,2,32,128,128]{3,4,1,2,0:T(8,128)(2,1)S(1)} fusion(f32[]{:T(128)} %bitcast.27, bf16[128,96,2,1,32]{0,1,2,3,4:T(8,128)(2,1)S(1)} %maximum_bitcast_fusion.2, bf16[128,96,2,1,32]{0,1,2,3,4:T(8,128)(2,1)S(1)} %copy-done.5, bf16[128,96,2,32,1]{0,3,2,1,4:T(8,128)(2,1)S(1)} %bitcast.83), kind=kOutput, calls=%fused_computation.23 | convolution fusion | flops 406323200 | bytes 6815748 | tf_op jit(solution)/shard_map/iscf,jscpf->pfij/dot_general | solution.py:16
  202.8 2.7 %fusion.17 = bf16[1,2,32,128,128]{3,4,1,2,0:T(8,128)(2,1)S(1)} fusion(f32[]{:T(128)} %bitcast.36, bf16[128,96,2,1,32]{0,1,2,3,4:T(8,128)(2,1)S(1)} %maximum_bitcast_fusion.3, bf16[128,96,2,1,32]{0,1,2,3,4:T(8,128)(2,1)S(1)} %copy.90, bf16[128,96,2,32,1]{0,3,2,1,4:T(8,128)(2,1)S(1)} %bitcast.84), kind=kOutput, calls=%fused_computation.24 | convolution fusion | flops 406323200 | bytes 6815748 | tf_op jit(solution)/shard_map/iscf,jscpf->pfij/dot_general | solution.py:16
  205.5 3.1 %maximum_bitcast_fusion = bf16[1,3,2,32,128,128]{4,5,2,3,1,0:T(8,128)(2,1)} fusion(bf16[1,2,32,128,128]{3,4,1,2,0:T(8,128)(2,1)S(1)} %fusion.17, bf16[1,2,32,128,128]{3,4,1,2,0:T(8,128)(2,1)S(1)} %fusion.16, bf16[1,2,32,128,128]{3,4,1,2,0:T(8,128)(2,1)S(1)} %copy-done.4), kind=kLoop, calls=%fused_computation.2 | loop fusion | flops 6291456 | bytes 12582912 | tf_op jit(solution)/shard_map/broadcast_in_dim | solution.py:61
  208.7 8.6 %copy.92 = bf16[1,3,2,32,128,128]{5,4,3,2,1,0:T(8,128)(2,1)} copy(bf16[1,3,2,32,128,128]{4,5,2,3,1,0:T(8,128)(2,1)} %maximum_bitcast_fusion) | data formatting | bytes 12582912 | tf_op jit(solution)/shard_map/broadcast_in_dim | solution.py:61
  (25 shorter events, 1.1 us)
Async XLA Ops:
  7.1 4.4 %copy-start.6 = (s32[8192]{0:T(1024)S(1)}, s32[8192]{0:T(1024)}, u32[]{:S(2)}) copy-start(s32[8192]{0:T(1024)} %param.4) | copy-start | bytes 98308
  7.1 25.1 %all-to-all-start = ((bf16[4,128,12,128]{1,3,2,0:T(8,128)(2,1)}), bf16[4,128,12,128]{1,3,2,0:T(8,128)(2,1)S(1)}, u32[]{:S(2)}, u32[]{:S(2)}) async-start(bf16[4,128,12,128]{1,3,2,0:T(8,128)(2,1)} %bitcast.8), calls=%async_computation | async-start | bytes 3145728 | tf_op jit(solution)/shard_map/all_to_all | solution.py:34
  52.0 66.9 %all-to-all-start.1 = ((bf16[64,3,48,128]{3,2,1,0:T(8,128)(2,1)}), bf16[64,3,48,128]{3,2,1,0:T(8,128)(2,1)S(1)}, u32[]{:S(2)}, u32[]{:S(2)}) async-start(bf16[64,3,48,128]{3,2,1,0:T(8,128)(2,1)} %scatter_fusion), calls=%async_computation.1 | async-start | bytes 4718592 | tf_op jit(solution)/shard_map/all_to_all | solution.py:46
  118.9 1.4 copy-start.1
  120.5 19.1 %copy-start.7 = (s32[1,3]{1,0:T(1,128)S(1)}, s32[1,3]{1,0:T(1,128)}, u32[]{:S(2)}) copy-start(s32[1,3]{1,0:T(1,128)} %param.5) | copy-start | bytes 40
  138.0 32.1 %collective-permute-start = (bf16[128,48,128]{2,1,0:T(8,128)(2,1)S(1)}, bf16[128,48,128]{2,1,0:T(8,128)(2,1)}, u32[]{:S(2)}, u32[]{:S(2)}) collective-permute-start(bf16[128,48,128]{2,1,0:T(8,128)(2,1)S(1)} %scatter_fusion.1), channel_id=1, source_target_pairs={{1,0},{2,1},{3,2},{4,3},{5,4},{6,5},{7,6},{8,7},{9,8},{10,9},{11,1... | collective-permute-start | bytes 4718600 | tf_op jit(solution)/shard_map/ppermute | solution.py:10
  143.3 50.5 %collective-permute-start.1 = (bf16[128,48,128]{2,1,0:T(8,128)(2,1)S(1)}, bf16[128,48,128]{2,1,0:T(8,128)(2,1)}, u32[]{:S(2)}, u32[]{:S(2)}) collective-permute-start(bf16[128,48,128]{2,1,0:T(8,128)(2,1)S(1)} %scatter_fusion.1), channel_id=1, source_target_pairs={{2,0},{3,1},{4,2},{5,3},{6,4},{7,5},{8,6},{9,7},{10,8},{11,9},{12,... | collective-permute-start | bytes 4718600 | tf_op jit(solution)/shard_map/ppermute | solution.py:10
  172.9 3.7 %copy-start = (bf16[128,48,128]{0,2,1:T(8,128)(2,1)S(1)}, bf16[128,48,128]{0,2,1:T(8,128)(2,1)}, u32[]{:S(2)}) copy-start(bf16[128,48,128]{0,2,1:T(8,128)(2,1)} %copy.80) | copy-start | bytes 4718596
  197.2 1.1 copy-start.2
  197.2 1.4 copy-start.3
  198.7 1.4 copy-start.5
  202.8 2.7 %copy-start.4 = (bf16[1,2,32,128,128]{3,4,1,2,0:T(8,128)(2,1)S(1)}, bf16[1,2,32,128,128]{3,4,1,2,0:T(8,128)(2,1)}, u32[]{:S(2)}) copy-start(bf16[1,2,32,128,128]{3,4,1,2,0:T(8,128)(2,1)} %fusion.15) | copy-start | bytes 6291460

commit v2 on v1

v2 whole, which is shorter than its diff:
```python
import functools

import jax
import jax.numpy as jnp
from jax import lax
from jax.experimental import pallas as pl
from jax.experimental.pallas import tpu as pltpu
from jax.sharding import PartitionSpec as P

MOST = 3
LANES = 128
MESH = pl.DeviceIdType.MESH
BF16 = jnp.bfloat16
F32 = jnp.float32


def iota(shape, axis):
    return lax.broadcasted_iota(jnp.int32, shape, axis)


def whiten_kernel(me, quads, raw_ref, table_ref, out_ref, pick_ref):
    rows = raw_ref.shape[1]
    slots = out_ref.shape[2]
    stations = rows // 2

    @pl.when(pl.program_id(0) == 0)
    def _():
        own = table_ref[pl.ds(me(), 1), :]
        across = jnp.broadcast_to(own, (stations, stations))
        down = jnp.transpose(across)
        same = (across == down) & (iota((stations, stations), 0) < iota((stations, stations), 1))
        rank = jnp.sum(same.astype(F32), axis=0, keepdims=True)
        slot = own.astype(F32) * MOST + rank
        spread = (lax.shift_right_logical(iota((stations, rows), 1), 1) == iota((stations, rows), 0)).astype(BF16)
        slot = jnp.broadcast_to(slot, (8, stations)).astype(BF16)
        wide = jnp.dot(slot, spread, preferred_element_type=F32)[0:1].astype(jnp.int32)
        place = wide * 2 + (iota((1, rows), 1) & 1)
        pick_ref[...] = (iota((slots, rows), 0) == place).astype(F32).astype(BF16)

    lane = iota((rows, LANES), 1)
    low = lane < 64
    even = (lane & 32) == 0
    odd_row = (iota((rows // 8, 8, LANES), 1) & 1) == 1
    pick = pick_ref[...]
    for quad in range(quads):
        white = []
        for part in range(4):
            x = raw_ref[quad * 4 + part].astype(F32)
            square = (x * x).reshape(rows // 8, 8, LANES)
            other = jnp.where(odd_row, pltpu.roll(square, 1, 1), pltpu.roll(square, 7, 1))
            power = (square + other).reshape(rows, LANES)
            level = jnp.sum(power, axis=1, keepdims=True) * (1.0 / LANES)
            white.append(x * lax.rsqrt(power + level + 1e-05))
        w0, w1, w2, w3 = white
        a0 = jnp.where(low, w0, pltpu.roll(w2, 64, 1))
        a2 = jnp.where(low, pltpu.roll(w0, 64, 1), w2)
        a1 = jnp.where(low, w1, pltpu.roll(w3, 64, 1))
        a3 = jnp.where(low, pltpu.roll(w1, 64, 1), w3)
        d0 = jnp.where(even, a0, pltpu.roll(a1, 32, 1))
        d1 = jnp.where(even, pltpu.roll(a0, 96, 1), a1)
        d2 = jnp.where(even, a2, pltpu.roll(a3, 32, 1))
        d3 = jnp.where(even, pltpu.roll(a2, 96, 1), a3)
        for half, (first, second) in enumerate(((d0, d1), (d2, d3))):
            both = jnp.concatenate([first.astype(BF16), second.astype(BF16)], axis=1)
            sent = jnp.dot(pick, both, preferred_element_type=F32).astype(BF16)
            out_ref[2 * half, quad] = sent[:, :LANES]
            out_ref[2 * half + 1, quad] = sent[:, LANES:]


def whiten(raw, table, me):
    segments, rows, _ = raw.shape
    quads = segments // 4
    step = 3
    slots = table.shape[0] * MOST * 2
    return pl.pallas_call(
        functools.partial(whiten_kernel, me, step),
        out_shape=jax.ShapeDtypeStruct((4, quads, slots, LANES), BF16),
        grid=(quads // step,),
        in_specs=[
            pl.BlockSpec((4 * step, rows, LANES), lambda i: (i, 0, 0)),
            pl.BlockSpec(table.shape, lambda i: (0, 0)),
        ],
        out_specs=pl.BlockSpec((4, step, slots, LANES), lambda i: (0, i, 0, 0)),
        scratch_shapes=[pltpu.VMEM((slots, rows), BF16)],
        name="whiten",
    )(raw, table)


def exchange_kernel(days, blocks, send, recv, send_sem, recv_sem):
    g = lax.axis_index("day")
    s = lax.axis_index("sta")
    own = pltpu.make_async_copy(send.at[g, :, s], recv.at[g, :, s], recv_sem.at[0])
    own.start()

    def start(d, b, kind):
        pltpu.make_async_remote_copy(
            src_ref=send.at[d, :, b],
            dst_ref=recv.at[g, :, s],
            send_sem=send_sem.at[kind],
            recv_sem=recv_sem.at[kind],
            device_id=(d, b),
            device_id_type=MESH,
        ).start()

    for turn in range(1, days):
        start(lax.rem(g + turn, days), s, 1)

    def step(t, carry):
        b = lax.rem(s + t, blocks)
        start(g, b, 0)
        for turn in range(1, days):
            start(lax.rem(g + turn, days), b, 1)
        return carry

    lax.fori_loop(1, blocks, step, 0)
    few = send.at[0, :, pl.ds(0, blocks - 1)]
    pltpu.make_async_copy(few, few, send_sem.at[0]).wait()
    rest = send.at[pl.ds(0, days - 1)]
    pltpu.make_async_copy(rest, rest, send_sem.at[1]).wait()
    pltpu.make_async_copy(recv.at[0], recv.at[0], recv_sem.at[0]).wait()
    rest = recv.at[pl.ds(0, days - 1)]
    pltpu.make_async_copy(rest, rest, recv_sem.at[1]).wait()


def exchange(send):
    days, _, blocks = send.shape[:3]
    return pl.pallas_call(
        functools.partial(exchange_kernel, days, blocks),
        out_shape=jax.ShapeDtypeStruct(send.shape, send.dtype),
        in_specs=[pl.BlockSpec(memory_space=pl.ANY)],
        out_specs=pl.BlockSpec(memory_space=pl.ANY),
        scratch_shapes=[pltpu.SemaphoreType.DMA((2,)), pltpu.SemaphoreType.DMA((2,))],
        compiler_params=pltpu.CompilerParams(has_side_effects=True),
        name="exchange",
    )(send)


def arrange_kernel(me, quads, recv_ref, table_ref, out_ref, pick_ref, wide_ref):
    slots = recv_ref.shape[1]
    shards, stations = table_ref.shape
    bins, depth, _ = out_ref.shape
    count = depth // 2

    @pl.when(pl.program_id(0) == 0)
    def _():
        mine = jnp.sum((table_ref[...] == me()).astype(F32), axis=1, keepdims=True)
        mine = jnp.broadcast_to(mine, (shards, LANES)).astype(BF16)
        lower = (iota((shards, shards), 1) < iota((shards, shards), 0)).astype(F32).astype(BF16)
        first = jnp.dot(lower, mine, preferred_element_type=F32)
        shard = iota((slots, shards), 1)
        row = iota((slots, shards), 0)
        member = ((row >= 6 * shard) & (row < 6 * shard + 6)).astype(F32).astype(BF16)
        first = jnp.dot(member, first.astype(BF16), preferred_element_type=F32).astype(jnp.int32)
        mine = jnp.dot(member, mine, preferred_element_type=F32).astype(jnp.int32)
        index = iota((shards, LANES), 0).astype(F32).astype(BF16)
        index = jnp.dot(member, index, preferred_element_type=F32).astype(jnp.int32)
        rest = iota((slots, LANES), 0) - 6 * index
        rank = lax.shift_right_logical(rest, 1)
        hit = (rank < mine) & (first + rank == iota((slots, LANES), 1))
        for part in range(2):
            chosen = (hit & ((rest & 1) == part)).astype(F32).astype(BF16)
            pick_ref[:, part * LANES:(part + 1) * LANES] = chosen

    pick = pick_ref[...]
    base = pl.program_id(0) * (4 * quads)
    for quad in range(quads):
        block = lax.dot_general(recv_ref[quad], pick, (((0,), (0,)), ((), ())), preferred_element_type=F32)
        for part in range(4):
            for kind in range(2):
                where = pl.ds(kind * count + base + quad * 4 + part, bins, stride=depth)
                wide_ref[where, :] = block[part * bins:(part + 1) * bins, kind * LANES:(kind + 1) * LANES]

    @pl.when(pl.program_id(0) == pl.num_programs(0) - 1)
    def _():
        def step(f, carry):
            out_ref[f] = wide_ref[pl.ds(pl.multiple_of(f * depth, depth), depth), :].astype(BF16)
            return carry

        lax.fori_loop(0, bins, step, 0)


def arrange(recv, table, me):
    total, slots, _ = recv.shape
    steps = 4
    quads = total // steps
    bins = LANES // 4
    depth = 2 * 4 * total
    return pl.pallas_call(
        functools.partial(arrange_kernel, me, quads),
        out_shape=jax.ShapeDtypeStruct((bins, depth, LANES), BF16),
        grid=(steps,),
        in_specs=[
            pl.BlockSpec((quads, slots, LANES), lambda i: (i, 0, 0)),
            pl.BlockSpec(table.shape, lambda i: (0, 0)),
        ],
        out_specs=pl.BlockSpec((bins, depth, LANES), lambda i: (0, 0, 0)),
        scratch_shapes=[pltpu.VMEM((slots, 2 * LANES), BF16), pltpu.VMEM((bins * depth, LANES), F32)],
        name="arrange",
    )(recv, table)


def neighbour_kernel(blocks, chunks, own, near, send_far, recv_far, send_near, recv_near):
    s = lax.axis_index("sta")
    g = lax.axis_index("day")
    odd = lax.rem(s, 2)
    partner = s + 1 - 2 * odd
    before = lax.rem(s + blocks - 2, blocks)
    after = lax.rem(s + 2, blocks)
    size = own.shape[0] // chunks

    barrier = pltpu.get_barrier_semaphore()
    for peer in (after, partner):
        pl.semaphore_signal(barrier, inc=1, device_id=(g, peer), device_id_type=MESH)
    pl.semaphore_wait(barrier, 2)

    def far(i):
        part = pl.ds(i * size, size)
        return pltpu.make_async_remote_copy(
            src_ref=own.at[part], dst_ref=near.at[1, part], send_sem=send_far.at[i], recv_sem=recv_far.at[i],
            device_id=(g, before), device_id_type=MESH)

    def close(i, source):
        part = pl.ds(i * size, size)
        return pltpu.make_async_remote_copy(
            src_ref=source.at[part], dst_ref=near.at[0, part], send_sem=send_near.at[i], recv_sem=recv_near.at[i],
            device_id=(g, partner), device_id_type=MESH)

    for i in range(chunks):
        far(i).start()

    @pl.when(odd == 1)
    def _():
        for i in range(chunks):
            close(i, own).start()
        for i in range(chunks):
            far(i).wait_recv()

    @pl.when(odd == 0)
    def _():
        for i in range(chunks):
            far(i).wait_recv()
            close(i, near.at[1]).start()

    for i in range(chunks):
        close(i, own).wait_recv()
    for i in range(chunks):
        close(i, own).wait_send()
        far(i).wait_send()


def neighbours(own, blocks):
    chunks = 8
    return pl.pallas_call(
        functools.partial(neighbour_kernel, blocks, chunks),
        out_shape=jax.ShapeDtypeStruct((2,) + own.shape, own.dtype),
        in_specs=[pl.BlockSpec(memory_space=pl.ANY)],
        out_specs=pl.BlockSpec(memory_space=pl.ANY),
        scratch_shapes=[pltpu.SemaphoreType.DMA((chunks,))] * 4,
        compiler_params=pltpu.CompilerParams(collective_id=1, has_side_effects=True),
        name="neighbours",
    )(own)


def correlate_kernel(scale, listed_ref, own_ref, near_ref, out_ref):
    bins, depth, width = own_ref.shape
    half = depth // 2
    gains = [listed_ref[0, o].astype(F32) * scale for o in range(3)]

    def one(f):
        own = own_ref[f]
        real, imag = own[:half], own[half:]
        left = jnp.concatenate(
            [jnp.concatenate([real, -imag], axis=1), jnp.concatenate([imag, real], axis=1)], axis=0)
        right = jnp.concatenate([own, near_ref[0, f], near_ref[1, f]], axis=1)
        product = lax.dot_general(left, right, (((0,), (0,)), ((), ())), preferred_element_type=F32)
        for o in range(3):
            for part in range(2):
                piece = product[part * width:(part + 1) * width, o * width:(o + 1) * width]
                out_ref[0, o, part, f] = (piece * gains[o]).astype(BF16)

    for f in range(bins):
        one(f)


def stack(own, near, listed, scale):
    bins, depth, width = own.shape
    step = 4
    return pl.pallas_call(
        functools.partial(correlate_kernel, scale),
        out_shape=jax.ShapeDtypeStruct((1, 3, 2, bins, width, width), BF16),
        grid=(bins // step,),
        in_specs=[
            pl.BlockSpec(memory_space=pltpu.SMEM),
            pl.BlockSpec((step, depth, width), lambda i: (i, 0, 0)),
            pl.BlockSpec((2, step, depth, width), lambda i: (0, i, 0, 0)),
        ],
        out_specs=pl.BlockSpec((1, 3, 2, step, width, width), lambda i: (0, 0, 0, i, 0, 0)),
        name="stack",
    )(listed, own, near)


def local(raw_spectra, station_block, pair_listed):
    blocks = lax.axis_size("sta")
    days = lax.axis_size("day")
    segments, stations, _, bins = raw_spectra.shape
    quads = segments // 4
    me = lambda: lax.axis_index("sta")
    table = station_block.reshape(blocks, stations)
    sent = whiten(raw_spectra.reshape(segments, 2 * stations, bins), table, me)
    got = exchange(sent.reshape(days, quads, blocks, MOST, 2, LANES))
    own = arrange(got.reshape(days * quads, blocks * MOST * 2, LANES), table, me)
    near = neighbours(own, blocks)
    scale = 1.0 / float(segments * days) ** 0.5
    return stack(own, near, pair_listed, scale)


def solution(mesh):
    in_specs = (P("day", "sta", None, None), P(), P("sta", None))
    out_specs = P("sta", None, None, "day", None, None)
    return jax.shard_map(local, mesh=mesh, in_specs=in_specs, out_specs=out_specs, check_vma=False)
```

time: 219 us -> 131 us (0.60)
  the two profiles are of different devices: /device:TPU:8 before, /device:TPU:1 now
where the time goes in v2:
time: 131 us; the launch traced here: 129 us
  Pallas kernels  129 us (98%)
    pallas_call x1, Pallas kernels, exchange(): pl.pallas_call(functools.partial(exchange_kernel, days, blocks), out_shap...  74.2 us
    pallas_call x1, Pallas kernels, neighbours(): pl.pallas_call(functools.partial(neighbour_kernel, blocks, chunks), out_s...  34.6 us
    pallas_call x1, Pallas kernels, stack(): pl.pallas_call(functools.partial(correlate_kernel, scale), out_shape=jax....  8.7 us
    pallas_call x1, Pallas kernels, arrange(): pl.pallas_call(functools.partial(arrange_kernel, me, quads), out_shape=ja...  6.51 us
    pallas_call x1, Pallas kernels, whiten(): pl.pallas_call(functools.partial(whiten_kernel, me, step), out_shape=jax....  5.2 us

profile of v2, /device:TPU:1, one launch (start us, length us, event | category | flops | bytes accessed | tf_op | source)
XLA Modules:
  0.0 129.2 jit_solution(8171637335201253584)
XLA Ops:
  0.0 5.2 %whiten.1 = bf16[4,6,384,128]{3,2,1,0:T(8,128)(2,1)} custom-call(bf16[24,256,128]{2,1,0:T(8,128)(2,1)} %bitcast.6, s32[64,128]{1,0:T(8,128)} %bitcast.7), custom_call_target="tpu_custom_call" | custom-call | tf_op jit(solution)/shard_map/whiten/pallas_call | solution.py:75
  5.2 74.2 %exchange.1 = bf16[4,6,64,3,2,128]{5,4,3,2,1,0:T(2,128)(2,1)} custom-call(bf16[4,6,64,3,2,128]{5,4,3,2,1,0:T(2,128)(2,1)} %bitcast.5), custom_call_target="tpu_custom_call" | custom-call | tf_op jit(solution)/shard_map/exchange/pallas_call | solution.py:127
  79.4 6.5 %arrange.1.own.own_ref = bf16[32,192,128]{2,1,0:T(8,128)(2,1)} custom-call(bf16[24,384,128]{2,1,0:T(8,128)(2,1)} %bitcast.4, s32[64,128]{1,0:T(8,128)} %bitcast.8), custom_call_target="tpu_custom_call" | custom-call | tf_op jit(solution)/shard_map/arrange/pallas_call | solution.py:188
  85.9 34.6 %neighbours.1.near_ref = bf16[2,32,192,128]{3,2,1,0:T(8,128)(2,1)} custom-call(bf16[32,192,128]{2,1,0:T(8,128)(2,1)} %arrange.1.own.own_ref), custom_call_target="tpu_custom_call" | custom-call | tf_op jit(solution)/shard_map/neighbours/pallas_call | solution.py:253
  120.5 8.7 %stack.1 = bf16[1,3,2,32,128,128]{5,4,3,2,1,0:T(8,128)(2,1)} custom-call(s32[1,3]{1,0:T(1,128)} %listed_ref.1, bf16[32,192,128]{2,1,0:T(8,128)(2,1)} %arrange.1.own.own_ref, bf16[2,32,192,128]{3,2,1,0:T(8,128)(2,1)} %neighbours.1.near_ref), custom_call_target="tpu_custom_call" | custom-call | tf_op jit(solution)/shard_map/stack/pallas_call | solution.py:288

commit v3 on v1

v3 whole, which is shorter than its diff:
```python
import functools

import jax
import jax.numpy as jnp
from jax import lax
from jax.experimental import pallas as pl
from jax.experimental.pallas import tpu as pltpu
from jax.sharding import PartitionSpec as P

MOST = 3
LANES = 128
MESH = pl.DeviceIdType.MESH
BF16 = jnp.bfloat16
F32 = jnp.float32


def iota(shape, axis):
    return lax.broadcasted_iota(jnp.int32, shape, axis)


def whiten_kernel(me, quads, raw_ref, table_ref, out_ref, pick_ref):
    rows = raw_ref.shape[1]
    slots = out_ref.shape[2]
    stations = rows // 2

    @pl.when(pl.program_id(0) == 0)
    def _():
        own = table_ref[pl.ds(me(), 1), :]
        across = jnp.broadcast_to(own, (stations, stations))
        down = jnp.transpose(across)
        same = (across == down) & (iota((stations, stations), 0) < iota((stations, stations), 1))
        rank = jnp.sum(same.astype(F32), axis=0, keepdims=True)
        slot = own.astype(F32) * MOST + rank
        spread = (lax.shift_right_logical(iota((stations, rows), 1), 1) == iota((stations, rows), 0)).astype(BF16)
        slot = jnp.broadcast_to(slot, (8, stations)).astype(BF16)
        wide = jnp.dot(slot, spread, preferred_element_type=F32)[0:1].astype(jnp.int32)
        place = wide * 2 + (iota((1, rows), 1) & 1)
        pick_ref[...] = (iota((slots, rows), 0) == place).astype(F32).astype(BF16)

    lane = iota((rows, LANES), 1)
    low = lane < 64
    even = (lane & 32) == 0
    odd_row = (iota((rows // 8, 8, LANES), 1) & 1) == 1
    pick = pick_ref[...]
    for quad in range(quads):
        white = []
        for part in range(4):
            x = raw_ref[quad * 4 + part].astype(F32)
            square = (x * x).reshape(rows // 8, 8, LANES)
            other = jnp.where(odd_row, pltpu.roll(square, 1, 1), pltpu.roll(square, 7, 1))
            power = (square + other).reshape(rows, LANES)
            level = jnp.sum(power, axis=1, keepdims=True) * (1.0 / LANES)
            white.append(x * lax.rsqrt(power + level + 1e-05))
        w0, w1, w2, w3 = white
        a0 = jnp.where(low, w0, pltpu.roll(w2, 64, 1))
        a2 = jnp.where(low, pltpu.roll(w0, 64, 1), w2)
        a1 = jnp.where(low, w1, pltpu.roll(w3, 64, 1))
        a3 = jnp.where(low, pltpu.roll(w1, 64, 1), w3)
        d0 = jnp.where(even, a0, pltpu.roll(a1, 32, 1))
        d1 = jnp.where(even, pltpu.roll(a0, 96, 1), a1)
        d2 = jnp.where(even, a2, pltpu.roll(a3, 32, 1))
        d3 = jnp.where(even, pltpu.roll(a2, 96, 1), a3)
        for half, (first, second) in enumerate(((d0, d1), (d2, d3))):
            both = jnp.concatenate([first.astype(BF16), second.astype(BF16)], axis=1)
            sent = jnp.dot(pick, both, preferred_element_type=F32).astype(BF16)
            out_ref[2 * half, quad] = sent[:, :LANES]
            out_ref[2 * half + 1, quad] = sent[:, LANES:]


def whiten(raw, table, me):
    segments, rows, _ = raw.shape
    quads = segments // 4
    step = 3
    slots = table.shape[0] * MOST * 2
    return pl.pallas_call(
        functools.partial(whiten_kernel, me, step),
        out_shape=jax.ShapeDtypeStruct((4, quads, slots, LANES), BF16),
        grid=(quads // step,),
        in_specs=[
            pl.BlockSpec((4 * step, rows, LANES), lambda i: (i, 0, 0)),
            pl.BlockSpec(table.shape, lambda i: (0, 0)),
        ],
        out_specs=pl.BlockSpec((4, step, slots, LANES), lambda i: (0, i, 0, 0)),
        scratch_shapes=[pltpu.VMEM((slots, rows), BF16)],
        name="whiten",
    )(raw, table)


def build_pick(me, table_ref, pick_ref):
    slots = pick_ref.shape[0]
    shards, stations = table_ref.shape
    mine = jnp.sum((table_ref[...] == me).astype(F32), axis=1, keepdims=True)
    mine = jnp.broadcast_to(mine, (shards, LANES)).astype(BF16)
    lower = (iota((shards, shards), 1) < iota((shards, shards), 0)).astype(F32).astype(BF16)
    first = jnp.dot(lower, mine, preferred_element_type=F32)
    shard = iota((slots, shards), 1)
    row = iota((slots, shards), 0)
    member = ((row >= 6 * shard) & (row < 6 * shard + 6)).astype(F32).astype(BF16)
    first = jnp.dot(member, first.astype(BF16), preferred_element_type=F32)
    mine = jnp.dot(member, mine, preferred_element_type=F32)
    index = iota((shards, LANES), 0).astype(F32).astype(BF16)
    index = jnp.dot(member, index, preferred_element_type=F32)
    rest = iota((slots, LANES), 0).astype(F32) - 6.0 * index
    imag = (iota((slots, LANES), 0) & 1) == 1
    rank = 0.5 * (rest - jnp.where(imag, 1.0, 0.0))
    hit = (rank < mine) & (first + rank == iota((slots, LANES), 1).astype(F32))
    for part in range(2):
        chosen = jnp.where(hit & (imag == (part == 1)), 1.0, 0.0).astype(BF16)
        pick_ref[:, part * LANES:(part + 1) * LANES] = chosen


def gather_kernel(dims, relayed, parts, send, table, own, near, recv, relay, fresh, wide, pick,
                  send_sem, recv_sem, relay_sem, pass_sem, local_sem, send_far, recv_far, send_near, recv_near):
    days, ny, nz = dims
    blocks = ny * nz * 2
    quads = recv.shape[1]
    bins = fresh.shape[1]
    g = lax.axis_index("day")
    s = lax.axis_index("sta")
    y = lax.div(s, 2 * nz)
    z = lax.rem(lax.div(s, 2), nz)
    c = lax.rem(s, 2)
    owners = [lax.rem(g + turn, days) for turn in range(days)]
    partner = s + 1 - 2 * c

    def at(dy, dz, dc):
        return lax.rem(y + dy, ny) * (2 * nz) + lax.rem(z + dz, nz) * 2 + lax.rem(c + dc, 2)

    barrier = pltpu.get_barrier_semaphore()

    def greet(t, carry):
        peer = lax.rem(s + t, blocks)
        for d in owners:
            pl.semaphore_signal(barrier, inc=1, device_id=(d, peer), device_id_type=MESH)
        return carry

    lax.fori_loop(1, blocks, greet, 0)
    for d in owners[1:]:
        pl.semaphore_signal(barrier, inc=1, device_id=(d, s), device_id_type=MESH)
    pl.semaphore_wait(barrier, days * blocks - 1)

    spans = [pl.ds(first, count) for first, count in parts]

    def post(i, d, kind, block, target, dst, sem):
        pltpu.make_async_remote_copy(
            src_ref=send.at[d, spans[i], block], dst_ref=dst, send_sem=send_sem.at[2 * i + kind], recv_sem=sem,
            device_id=(d, target), device_id_type=MESH).start()

    def post_all(i, block, target, dst, sem, turns):
        for turn in turns:
            post(i, owners[turn], min(turn, 1), block, target, dst, sem)

    def post_half(i):
        def step(t, carry):
            block = at(lax.div(t, 2), nz // 2, lax.rem(t, 2))
            target = at(lax.div(t, 2), nz // 2 - 1, lax.rem(t, 2)) if relayed else block
            dst = relay.at[g, spans[i], y, c] if relayed else recv.at[g, spans[i], y, z, c]
            post_all(i, block, target, dst, relay_sem.at[i] if relayed else recv_sem.at[i], range(days))
            return carry

        lax.fori_loop(0, 2 * ny, step, 0)

    def post_rest(i):
        dst = recv.at[g, spans[i], y, z, c]

        def step(u, carry):
            k = lax.div(u, 2 * ny) + 1
            t = lax.rem(u, 2 * ny) + 2
            dz = lax.rem(nz + nz // 2 + lax.div(k + 1, 2) * (1 - 2 * lax.rem(k, 2)), nz)
            block = at(lax.div(t, 2), dz, lax.rem(t, 2) + 1)
            post_all(i, block, block, dst, recv_sem.at[i], range(days))
            return carry

        lax.fori_loop(0, 2 * ny * (nz - 1) - 1, step, 0)
        post_all(i, s, s, dst, recv_sem.at[i], range(1, days))

    def keep(i):
        pltpu.make_async_copy(send.at[g, spans[i], s], recv.at[g, spans[i], y, z, c], recv_sem.at[i]).start()

    def hand_on(i):
        return pltpu.make_async_remote_copy(
            src_ref=relay.at[:, spans[i]], dst_ref=recv.at[:, spans[i], :, lax.rem(z + nz // 2 + 1, nz)],
            send_sem=pass_sem.at[i], recv_sem=recv_sem.at[i], device_id=(g, at(0, 1, 0)), device_id_type=MESH)

    def await_relay(i):
        held = relay.at[:, spans[i]]
        pltpu.make_async_copy(held, held, relay_sem.at[i]).wait()

    def far(j):
        return pltpu.make_async_remote_copy(
            src_ref=own.at[j], dst_ref=near.at[1, j], send_sem=send_far.at[j], recv_sem=recv_far.at[j],
            device_id=(g, lax.rem(s + blocks - 2, blocks)), device_id_type=MESH)

    def close(j, source):
        return pltpu.make_async_remote_copy(
            src_ref=source.at[j], dst_ref=near.at[0, j], send_sem=send_near.at[j], recv_sem=recv_near.at[j],
            device_id=(g, partner), device_id_type=MESH)

    dense = recv.reshape(days, quads, blocks * MOST * 2, LANES)

    def arrange(i):
        held = recv.at[:, spans[i]]
        pltpu.make_async_copy(held, held, recv_sem.at[i]).wait()
        first, count = parts[i]
        for j in range(first, first + count):
            for day in range(days):
                block = lax.dot_general(dense[day, j], pick[...], (((0,), (0,)), ((), ())), preferred_element_type=F32)
                for part in range(4):
                    for kind in range(2):
                        where = pl.ds(kind * 4 * days + day * 4 + part, bins, stride=8 * days)
                        wide[where, :] = block[part * bins:(part + 1) * bins, kind * LANES:(kind + 1) * LANES]
            fresh[j] = wide[...].reshape(bins, 8 * days, LANES).astype(BF16)
            pltpu.make_async_copy(fresh.at[j], own.at[j], local_sem.at[j]).start()
        for j in range(first, first + count):
            pltpu.make_async_copy(fresh.at[j], own.at[j], local_sem.at[j]).wait()
            far(j).start()

    n = len(parts)
    if relayed:
        post_half(0)
        post_rest(0)
        keep(0)
        for i in range(1, n):
            post_half(i)
            await_relay(i - 1)
            hand_on(i - 1).start()
            post_rest(i)
            keep(i)
            if i == 1:
                build_pick(s, table, pick)
        for i in range(n):
            if i == 1 or n == 1:
                await_relay(n - 1)
                hand_on(n - 1).start()
            arrange(i)
    else:
        for i in range(n):
            post_half(i)
            post_rest(i)
            keep(i)
        build_pick(s, table, pick)
        for i in range(n):
            arrange(i)

    @pl.when(c == 1)
    def _():
        for j in range(quads):
            close(j, own).start()
        for j in range(quads):
            far(j).wait_recv()

    @pl.when(c == 0)
    def _():
        for j in range(quads):
            far(j).wait_recv()
            close(j, near.at[1]).start()

    for j in range(quads):
        close(j, own).wait_recv()
    for i in range(n):
        few = send.at[0, spans[i], pl.ds(0, blocks - 1)]
        pltpu.make_async_copy(few, few, send_sem.at[2 * i]).wait()
        rest = send.at[pl.ds(0, days - 1), spans[i]]
        pltpu.make_async_copy(rest, rest, send_sem.at[2 * i + 1]).wait()
        if relayed:
            hand_on(i).wait_send()
    for j in range(quads):
        close(j, own).wait_send()
        far(j).wait_send()


def gather(send, table, dims, relayed, parts):
    days, ny, nz = dims
    quads, blocks = send.shape[1:3]
    bins = LANES // 4
    n = len(parts)
    tail = (MOST, 2, LANES)
    piece = (quads, bins, 8 * days, LANES)
    dma = pltpu.SemaphoreType.DMA
    return pl.pallas_call(
        functools.partial(gather_kernel, dims, relayed, parts),
        out_shape=(jax.ShapeDtypeStruct(piece, BF16), jax.ShapeDtypeStruct((2,) + piece, BF16)),
        in_specs=[pl.BlockSpec(memory_space=pl.ANY), pl.BlockSpec(memory_space=pltpu.VMEM)],
        out_specs=(pl.BlockSpec(memory_space=pl.ANY), pl.BlockSpec(memory_space=pl.ANY)),
        scratch_shapes=[
            pltpu.VMEM((days, quads, ny, nz, 2) + tail, BF16),
            pltpu.VMEM((days, quads, ny, 2) + tail, BF16),
            pltpu.VMEM(piece, BF16),
            pltpu.VMEM((bins * 8 * days, LANES), F32),
            pltpu.VMEM((blocks * MOST * 2, 2 * LANES), BF16),
            dma((2 * n,)), dma((n,)), dma((n,)), dma((n,)), dma((quads,)),
            dma((quads,)), dma((quads,)), dma((quads,)), dma((quads,)),
        ],
        compiler_params=pltpu.CompilerParams(collective_id=0, has_side_effects=True),
        name="gather",
    )(send, table)


def correlate_kernel(scale, listed_ref, own_ref, near_ref, out_ref):
    quads, bins, depth, width = own_ref.shape
    half = depth // 2
    gains = [listed_ref[0, o].astype(F32) * scale for o in range(3)]
    for f in range(bins):
        own = [own_ref[j, f] for j in range(quads)]
        left = []
        for piece in own:
            real, imag = piece[:half], piece[half:]
            left.append(jnp.concatenate([real, -imag], axis=1))
            left.append(jnp.concatenate([imag, real], axis=1))
        right = [jnp.concatenate(own, axis=0)]
        for o in range(2):
            right.append(jnp.concatenate([near_ref[o, j, f] for j in range(quads)], axis=0))
        product = lax.dot_general(
            jnp.concatenate(left, axis=0), jnp.concatenate(right, axis=1), (((0,), (0,)), ((), ())),
            preferred_element_type=F32)
        for o in range(3):
            for part in range(2):
                piece = product[part * width:(part + 1) * width, o * width:(o + 1) * width]
                out_ref[0, o, part, f] = (piece * gains[o]).astype(BF16)


def stack(own, near, listed, scale):
    quads, bins, depth, width = own.shape
    step = 4
    return pl.pallas_call(
        functools.partial(correlate_kernel, scale),
        out_shape=jax.ShapeDtypeStruct((1, 3, 2, bins, width, width), BF16),
        grid=(bins // step,),
        in_specs=[
            pl.BlockSpec(memory_space=pltpu.SMEM),
            pl.BlockSpec((quads, step, depth, width), lambda i: (0, i, 0, 0)),
            pl.BlockSpec((2, quads, step, depth, width), lambda i: (0, 0, i, 0, 0)),
        ],
        out_specs=pl.BlockSpec((1, 3, 2, step, width, width), lambda i: (0, 0, 0, i, 0, 0)),
        name="stack",
    )(listed, own, near)


RELAYED = True
PARTS = ((0, 3), (3, 2), (5, 1))


def local(raw_spectra, station_block, pair_listed):
    blocks = lax.axis_size("sta")
    days = lax.axis_size("day")
    segments, stations, _, bins = raw_spectra.shape
    quads = segments // 4
    me = lambda: lax.axis_index("sta")
    table = station_block.reshape(blocks, stations)
    sent = whiten(raw_spectra.reshape(segments, 2 * stations, bins), table, me)
    sent = sent.reshape(days, quads, blocks, MOST, 2, LANES)
    own, near = gather(sent, table, (days, blocks // 16, 8), RELAYED, PARTS)
    scale = 1.0 / float(segments * days) ** 0.5
    return stack(own, near, pair_listed, scale)


def solution(mesh):
    in_specs = (P("day", "sta", None, None), P(), P("sta", None))
    out_specs = P("sta", None, None, "day", None, None)
    return jax.shard_map(local, mesh=mesh, in_specs=in_specs, out_specs=out_specs, check_vma=False)
```

time: 219 us -> 113 us (0.52)
  the two profiles are of different devices: /device:TPU:8 before, /device:TPU:1 now
where the time goes in v3:
time: 113 us
  Pallas kernels  113 us (100%)
    pallas_call x1, Pallas kernels, gather(): pl.pallas_call(functools.partial(gather_kernel, dims, relayed, parts), ou...  98.9 us
    pallas_call x1, Pallas kernels, stack(): pl.pallas_call(functools.partial(correlate_kernel, scale), out_shape=jax....  8.71 us
    pallas_call x1, Pallas kernels, whiten(): pl.pallas_call(functools.partial(whiten_kernel, me, step), out_shape=jax....  5.2 us

profile of v3, /device:TPU:1, one launch (start us, length us, event | category | flops | bytes accessed | tf_op | source)
XLA Modules:
  0.0 112.8 jit_solution(17552464867859948843)
XLA Ops:
  0.0 5.2 %whiten.1 = bf16[4,6,384,128]{3,2,1,0:T(8,128)(2,1)} custom-call(bf16[24,256,128]{2,1,0:T(8,128)(2,1)} %bitcast.4, s32[64,128]{1,0:T(8,128)} %bitcast.5), custom_call_target="tpu_custom_call" | custom-call | tf_op jit(solution)/shard_map/whiten/pallas_call | solution.py:75
  5.2 98.9 %gather.1 = (bf16[6,32,32,128]{3,2,1,0:T(8,128)(2,1)}, bf16[2,6,32,32,128]{4,3,2,1,0:T(8,128)(2,1)}) custom-call(bf16[4,6,64,3,2,128]{5,4,3,2,1,0:T(2,128)(2,1)} %bitcast.3, s32[64,128]{1,0:T(8,128)} %bitcast.6), custom_call_target="tpu_custom_call" | custom-call | tf_op jit(solution)/shard_map/gather/pallas_call | solution.py:280
  104.1 8.7 %stack.1 = bf16[1,3,2,32,128,128]{5,4,3,2,1,0:T(8,128)(2,1)} custom-call(s32[1,3]{1,0:T(1,128)} %listed_ref.1, bf16[6,32,32,128]{3,2,1,0:T(8,128)(2,1)} %get-tuple-element.7.own_ref, bf16[2,6,32,32,128]{4,3,2,1,0:T(8,128)(2,1)} %get-tuple-element.8.near_ref), custom_call_target="tpu_custom_call" | custom-call | tf_op jit(solution)/shard_map/stack/pallas_call | solution.py:325
